TPU v7x, 128 devices: a whole 4x4x4 slice. The times are simulated.
128 devices in a mesh: node: 16 (over z, y), local: 8 (over x, core).
Axes of the slice: x: 4, y: 4, z: 4, core: 2. Of those that a mesh axis runs over, the one named last changes fastest.
Arguments:
- tokens: bfloat16 [16384, 3584], P(('node', 'local')), may hold values from -6 to 6
- expert_ids: int32 [16384, 8], P(('node', 'local')), may hold values from 0 to 127, as said below
- gate_quanta: int32 [16384, 8], P(('node', 'local')), may hold values from 1 to 65535
- w_gate: bfloat16 [128, 3584, 1024], P(('node', 'local')), may hold values from -0.09375 to 0.09375
- w_up: bfloat16 [128, 3584, 1024], P(('node', 'local')), may hold values from -0.09375 to 0.09375
- w_down: bfloat16 [128, 1024, 3584], P(('node', 'local')), may hold values from -0.1875 to 0.1875
Outputs:
- mixed_rows: bfloat16 [16384, 3584], P(('node', 'local'))
Inputs may be any that keep to these rules, and one draw needn't show every extreme that they name: `expert_ids`: each row names 8 different experts that lie in at most 4 node groups, experts g * 8 to (g + 1) * 8 - 1 forming group g; in the rows of one device no expert is named more than 10 times and no node group is chosen by more than 32 tokens.
All inputs are finite; a program needn't handle non-finite values.
Results may differ from a plain program's by a relative error of at most 0.0058.
Values may be sent and summed in bfloat16 or wider, within the bound.
No kernel may reach another device: no remote copies, remote signals or barrier semaphores. Data moves between devices by JAX's collectives and lax.ppermute only.
A program may use at most 192 MiB of HBM per device.

v0:
```python
import jax
import jax.numpy as jnp
from jax import lax
from jax.sharding import PartitionSpec as P

ROUTED_SCALE = 2.5


def on_device(tokens, expert_ids, gate_quanta, w_gate, w_up, w_down):
    tok_rows, top_count = expert_ids.shape
    model_width = tokens.shape[1]
    node_count = lax.axis_size("node")
    local_count = lax.axis_size("local")
    experts = node_count * local_count
    mean_rows = tok_rows * top_count // experts
    most_slots = mean_rows + max(1, mean_rows // 4)
    capacity = tok_rows * top_count * 9 // 8
    quanta = gate_quanta.astype(jnp.float32)
    gate_scale = ROUTED_SCALE * quanta / jnp.sum(quanta, axis=1, keepdims=True)
    onehot = (expert_ids[:, :, None] == jnp.arange(experts, dtype=jnp.int32)[None, None, :]).astype(
        jnp.int32
    )
    per_token = jnp.sum(onehot, axis=1)
    earlier_count = jnp.cumsum(per_token, axis=0) - per_token
    slot_rank = jnp.sum(onehot * earlier_count[:, None, :], axis=2)
    counts = jnp.sum(per_token, axis=0)
    everyone = lax.all_gather(counts[None, :], ("node", "local"), axis=0, tiled=True)
    device_index = lax.axis_index("node") * local_count + lax.axis_index("local")
    lower_mask = (jnp.arange(experts, dtype=jnp.int32) < device_index).astype(jnp.int32)
    offsets = jnp.sum(everyone * lower_mask[:, None], axis=0)
    position = jnp.sum(onehot * offsets[None, None, :], axis=2) + slot_rank
    kept_mask = position < capacity
    weight_mix = jnp.where(kept_mask, gate_scale, jnp.zeros_like(gate_scale))
    dump_slot = experts * most_slots
    slot_index = jnp.where(kept_mask, expert_ids * most_slots + slot_rank, dump_slot)
    token_index = jnp.broadcast_to(jnp.arange(tok_rows, dtype=jnp.int32)[:, None], expert_ids.shape)
    source_table = (
        jnp.zeros((dump_slot + 1,), jnp.int32)
        .at[slot_index.reshape(-1)]
        .set(token_index.reshape(-1))[:dump_slot]
    )
    live_slots = (
        jnp.zeros((dump_slot + 1,), jnp.bool_).at[slot_index.reshape(-1)].set(True)[:dump_slot]
    )
    outgoing = jnp.where(live_slots[:, None], tokens[source_table], jnp.zeros((), tokens.dtype))
    arrived = lax.all_to_all(
        outgoing.reshape(experts, most_slots, model_width),
        ("node", "local"),
        split_axis=0,
        concat_axis=0,
        tiled=True,
    )
    arrived_flat = arrived.reshape(dump_slot, model_width)
    gate_part = jnp.dot(arrived_flat, w_gate[0], preferred_element_type=jnp.float32)
    up_part = jnp.dot(arrived_flat, w_up[0], preferred_element_type=jnp.float32)
    hidden = (jax.nn.silu(gate_part) * up_part).astype(jnp.bfloat16)
    expert_out = jnp.dot(hidden, w_down[0], preferred_element_type=jnp.float32).astype(jnp.bfloat16)
    returned = lax.all_to_all(
        expert_out.reshape(experts, most_slots, model_width),
        ("node", "local"),
        split_axis=0,
        concat_axis=0,
        tiled=True,
    )
    returned_flat = returned.reshape(dump_slot, model_width)
    gather_index = jnp.minimum(slot_index, dump_slot - 1)
    picked = returned_flat[gather_index]
    mixed_rows = jnp.sum(weight_mix[:, :, None] * picked.astype(jnp.float32), axis=1)
    return mixed_rows.astype(jnp.bfloat16)


def solution(mesh):
    in_specs = (
        P(("node", "local"), None),
        P(("node", "local"), None),
        P(("node", "local"), None),
        P(("node", "local"), None, None),
        P(("node", "local"), None, None),
        P(("node", "local"), None, None),
    )
    out_specs = P(("node", "local"), None)
    return jax.shard_map(
        on_device, mesh=mesh, in_specs=in_specs, out_specs=out_specs, check_vma=False
    )
```

profile of v0, /device:TPU:84, one launch (start us, length us, event | category | flops | bytes accessed | tf_op | source)
XLA Modules:
  0.0 573.8 jit_solution(4487164872582036108)
XLA Ops:
  0.0 0.9 copy.24
  0.9 0.2 convert_reduce_fusion
  1.1 0.2 reduce_window_sum.11
  1.3 29.8 %all-gather.1 = s32[128,1,128]{2,1,0:T(1,128)S(1)} all-gather(s32[1,1,128]{2,1,0:T(1,128)S(1)} %bitcast.25), channel_id=2, replica_groups=mesh['node'=16,'local'=8] {'node','local'}, dimensions={0}, use_global_device_ids=true | all-gather | bytes 66048 | tf_op jit(solution)/shard_map/all_gather | solution.py:27
  31.2 4.5 select_reduce_fusion
  35.9 0.7 convert_reduce_fusion.2
  36.6 0.7 divide_select_fusion
  37.3 0.7 compare_select_fusion.2
  38.3 4.3 scatter_custom_fusion.1
  42.7 7.8 %gather_fusion = bf16[1280,3584]{1,0:T(8,128)(2,1)} fusion(bf16[128,3584]{1,0:T(8,128)(2,1)S(1)} %copy-done, s32[2048]{0:T(1024)S(1)} %pad_clamp_fusion), kind=kCustom, calls=%fused_computation | custom fusion | bytes 18355200 | tf_op jit(solution)/shard_map/gather | solution.py:45
  50.5 14.2 %gather.9 = bf16[128,10,3584]{2,1,0:T(8,128)(2,1)} reshape(bf16[1280,3584]{1,0:T(8,128)(2,1)} %gather_fusion) | data formatting | bytes 18350080 | tf_op jit(solution)/shard_map/gather | solution.py:45
  64.7 4.3 scatter_custom_fusion
  69.2 6.1 %broadcast_select_fusion = bf16[128,10,3584]{2,1,0:T(8,128)(2,1)S(1)} fusion(bf16[128,10,3584]{2,1,0:T(8,128)(2,1)} %gather.9, pred[128,10]{1,0:T(8,128)(4,1)S(1)} %broadcast_in_dim.60), kind=kLoop, calls=%fused_computation.7 | loop fusion | flops 4587520 | bytes 18351360 | tf_op jit(solution)/shard_map/jit(_where)/select_n | solution.py:45
  75.3 169.3 %all_to_all.10 = bf16[128,10,3584]{2,1,0:T(8,128)(2,1)} all-to-all(bf16[128,10,3584]{2,1,0:T(8,128)(2,1)S(1)} %broadcast_select_fusion), channel_id=1, replica_groups=mesh['node'=16,'local'=8] {'node','local'}, dimensions={0} | all-to-all | bytes 18350080 | tf_op jit(solution)/shard_map/all_to_all | solution.py:46
  244.6 14.6 %reshape.72 = bf16[1280,3584]{1,0:T(8,128)(2,1)} reshape(bf16[128,10,3584]{2,1,0:T(8,128)(2,1)} %all_to_all.10) | data formatting | bytes 18350080 | tf_op jit(solution)/shard_map/reshape | solution.py:53
  259.2 13.4 %fusion.2 = f32[1280,1024]{1,0:T(8,128)S(1)} fusion(bf16[1280,3584]{1,0:T(8,128)(2,1)} %reshape.72, bf16[1,3584,1024]{2,1,0:T(8,128)(2,1)} %param.10), kind=kOutput, calls=%fused_computation.9 | convolution fusion | flops 9395240960 | bytes 21757952 | tf_op jit(solution)/shard_map/dot_general | solution.py:55
  272.6 12.7 %multiply_convert_fusion = bf16[1280,1024]{1,0:T(8,128)(2,1)S(1)} fusion(f32[1280,1024]{1,0:T(8,128)S(1)} %fusion.2, bf16[1280,3584]{1,0:T(8,128)(2,1)S(1)} %copy-done.2, bf16[1,3584,1024]{2,1,0:T(8,128)(2,1)} %param.9), kind=kOutput, calls=%fused_computation.13 | convolution fusion | flops 9403105280 | bytes 24379392 | tf_op jit(solution)/shard_map/dot_general | solution.py:54
  285.4 14.9 %convolution_convert_fusion = bf16[1280,3584]{1,0:T(8,128)(2,1)} fusion(bf16[1280,1024]{1,0:T(8,128)(2,1)S(1)} %multiply_convert_fusion, bf16[1,1024,3584]{2,1,0:T(8,128)(2,1)} %param.11), kind=kOutput, calls=%fused_computation.4 | convolution fusion | flops 9399828480 | bytes 19136512 | tf_op jit(solution)/shard_map/dot_general | solution.py:57
  300.3 14.2 %reshape.73 = bf16[128,10,3584]{2,1,0:T(8,128)(2,1)} reshape(bf16[1280,3584]{1,0:T(8,128)(2,1)} %convolution_convert_fusion) | data formatting | bytes 18350080 | tf_op jit(solution)/shard_map/reshape | solution.py:59
  314.5 11.5 %all-to-all-start.1 = ((bf16[128,10,3584]{2,1,0:T(8,128)(2,1)}), bf16[128,10,3584]{2,1,0:T(8,128)(2,1)}, u32[]{:S(2)}, u32[]{:S(2)}) async-start(bf16[128,10,3584]{2,1,0:T(8,128)(2,1)} %reshape.73), calls=%async_computation.1 | async-start | bytes 29360128 | tf_op jit(solution)/shard_map/all_to_all | solution.py:58
  326.3 203.4 %all-to-all-done.1 = bf16[128,10,3584]{2,1,0:T(8,128)(2,1)} async-done(((bf16[128,10,3584]{2,1,0:T(8,128)(2,1)}), bf16[128,10,3584]{2,1,0:T(8,128)(2,1)}, u32[]{:S(2)}, u32[]{:S(2)}) %all-to-all-start.1) | async-done | bytes 9175072 | tf_op jit(solution)/shard_map/all_to_all | solution.py:58
  529.8 14.6 %reshape.74 = bf16[1280,3584]{1,0:T(8,128)(2,1)} reshape(bf16[128,10,3584]{2,1,0:T(8,128)(2,1)} %all-to-all-done.1) | data formatting | bytes 18350080 | tf_op jit(solution)/shard_map/reshape | solution.py:65
  544.4 18.7 %gather_fusion.1 = bf16[1024,3584]{1,0:T(8,128)(2,1)} fusion(bf16[1280,3584]{1,0:T(8,128)(2,1)} %reshape.74, s32[1024]{0:T(1024)S(1)} %broadcast_clamp_fusion), kind=kCustom, calls=%fused_computation.1 | custom fusion | bytes 14684160 | tf_op jit(solution)/shard_map/gather | solution.py:67
  563.1 10.7 %fusion = bf16[128,3584]{1,0:T(8,128)(2,1)} fusion(bf16[1024,3584]{1,0:T(8,128)(2,1)} %gather_fusion.1, f32[128,8]{1,0:T(8,128)S(1)} %copy.27), kind=kLoop, calls=%fused_computation.6 | loop fusion | flops 10551296 | bytes 8261632 | tf_op jit(solution)/shard_map/reduce_sum | solution.py:68
  (24 shorter events, 1.0 us)
Async XLA Ops:
  0.0 42.7 %copy-start = (bf16[128,3584]{1,0:T(8,128)(2,1)S(1)}, bf16[128,3584]{1,0:T(8,128)(2,1)}, u32[]{:S(2)}) copy-start(bf16[128,3584]{1,0:T(8,128)(2,1)} %param.6) | copy-start | bytes 2752516
  259.2 13.5 %copy-start.2 = (bf16[1280,3584]{1,0:T(8,128)(2,1)S(1)}, bf16[1280,3584]{1,0:T(8,128)(2,1)}, u32[]{:S(2)}) copy-start(bf16[1280,3584]{1,0:T(8,128)(2,1)} %reshape.72) | copy-start | bytes 27525124
  314.5 215.3 %all-to-all-start.1 = ((bf16[128,10,3584]{2,1,0:T(8,128)(2,1)}), bf16[128,10,3584]{2,1,0:T(8,128)(2,1)}, u32[]{:S(2)}, u32[]{:S(2)}) async-start(bf16[128,10,3584]{2,1,0:T(8,128)(2,1)} %reshape.73), calls=%async_computation.1 | async-start | bytes 29360128 | tf_op jit(solution)/shard_map/all_to_all | solution.py:58
  544.4 29.4 %copy-start.1 = (bf16[128,3584]{1,0:T(8,128)(2,1)S(1)}, bf16[128,3584]{1,0:T(8,128)(2,1)}, u32[]{:S(2)}) copy-start(bf16[128,3584]{1,0:T(8,128)(2,1)} %param.6) | copy-start | bytes 2752516
where the time goes:
time: 576 us; the launch traced here: 574 us
  waiting for transfers between devices  203 us (35%)
  blocking collectives  199 us (35%)
  local copies, waits for them, and re-layouts  94.5 us (16%)
  matrix products  41.1 us (7%)
  other arithmetic  24 us (4%)
  starting transfers between devices  11.5 us (2%)
    all_to_all x1, waiting for transfers between devices, on_device(): lax.all_to_all(expert_out.reshape(experts, most_slots, model_width), ('no...  203 us
    all_to_all x1, blocking collectives, on_device(): lax.all_to_all(outgoing.reshape(experts, most_slots, model_width), ('node...  169 us
    all_gather x1, blocking collectives, on_device(): lax.all_gather(counts[None, :], ('node', 'local'), axis=0, tiled=True)  29.8 us
    gather x2, local copies, waits for them, and re-layouts, on_device(): tokens[source_table]  22 us
    gather x1, local copies, waits for them, and re-layouts, on_device(): picked = returned_flat[gather_index]  18.7 us
    dot_general x1, matrix products, on_device(): jnp.dot(hidden, w_down[0], preferred_element_type=jnp.float32)  14.9 us
    reshape x1, local copies, waits for them, and re-layouts, on_device(): arrived_flat = arrived.reshape(dump_slot, model_width)  14.6 us
    reshape x1, local copies, waits for them, and re-layouts, on_device(): returned_flat = returned.reshape(dump_slot, model_width)  14.6 us
  transfers between devices with their start and end apart: 1, of which 1 were waited for; matrix products, arithmetic and copies ran while one was open for 0% of the time, Pallas kernels for 0%

commit v1 on v0

v1 whole, which is shorter than its diff:
```python
import jax
import jax.numpy as jnp
from jax import lax
from jax.experimental import pallas as pl
from jax.experimental.pallas import tpu as pltpu
from jax.sharding import PartitionSpec as P

ROUTED_SCALE = 2.5
SUB = 8
EXTRA = 2
PIECES = 4
LANES = 128
MARK = 1048576.0
VMEM_BYTES = 58 * 1024 * 1024
BF16 = jnp.bfloat16
F32 = jnp.float32


def _iota(shape, dim):
    return lax.broadcasted_iota(jnp.int32, shape, dim)


def _dot(a, b):
    return jnp.dot(a, b, preferred_element_type=F32)


def _chosen(ids_t_ref, experts):
    top, toks = ids_t_ref.shape
    row = _iota((experts, toks), 0)
    total = jnp.zeros((experts, toks), F32)
    for k in range(top):
        total = total + (ids_t_ref[k : k + 1, :] == row).astype(F32)
    return total


def _ranks(chosen):
    toks = chosen.shape[1]
    before = (_iota((toks, toks), 0) < _iota((toks, toks), 1)).astype(BF16)
    return jnp.where(chosen > 0, _dot(chosen.astype(BF16), before), -1.0)


def dispatch_body(ids_t_ref, tokens_ref, out_ref, rank_ref):
    toks, width = tokens_ref.shape
    experts = rank_ref.shape[0]
    rows = out_ref.shape[0]
    piece = width // PIECES

    @pl.when(pl.program_id(0) == 0)
    def _():
        rank_ref[...] = _ranks(_chosen(ids_t_ref, experts)).astype(BF16)

    row = _iota((rows, experts), 0) + pl.program_id(0) * rows
    spread = (row // SUB == _iota((rows, experts), 1)).astype(BF16)
    rank = _dot(spread, rank_ref[...]).astype(jnp.int32)
    sub = _iota((rows, toks), 0) % SUB
    pick = (rank == sub).astype(BF16)
    main = _dot(pick, tokens_ref[...])
    filled = jnp.sum(pick.astype(F32), axis=1, keepdims=True)
    out_ref[:, 0:LANES] = jnp.where(filled > 0, main[:, 0:LANES], MARK).astype(BF16)
    out_ref[:, LANES:width] = main[:, LANES:].astype(BF16)
    extra = rank == SUB + sub // PIECES
    acc = jnp.zeros((rows, piece), F32)
    for c in range(PIECES):
        part = (extra & (sub % PIECES == c)).astype(BF16)
        acc = acc + _dot(part, tokens_ref[:, c * piece : (c + 1) * piece])
    filled = jnp.sum(extra.astype(F32), axis=1, keepdims=True)
    out_ref[:, width : width + LANES] = jnp.where(filled > 0, acc[:, 0:LANES], MARK).astype(BF16)
    out_ref[:, width + LANES :] = acc[:, LANES:].astype(BF16)


def dispatch(ids_t, tokens, experts):
    toks, width = tokens.shape
    rows = 256
    wide = width + width // PIECES
    return pl.pallas_call(
        dispatch_body,
        grid=(experts * SUB // rows,),
        in_specs=[
            pl.BlockSpec(ids_t.shape, lambda i: (0, 0)),
            pl.BlockSpec(tokens.shape, lambda i: (0, 0)),
        ],
        out_specs=pl.BlockSpec((rows, wide), lambda i: (i, 0)),
        out_shape=jax.ShapeDtypeStruct((experts * SUB, wide), BF16),
        scratch_shapes=[pltpu.VMEM((experts, toks), BF16)],
        compiler_params=pltpu.CompilerParams(vmem_limit_bytes=VMEM_BYTES),
        name="dispatch",
    )(ids_t, tokens)


W_CHUNKS = 8


def expert_body(capacity, arrived_ref, gate_hbm, up_hbm, down_hbm, out_ref, gate_w, up_w, down_w, x_ref, g_ref, u_ref, h_ref, seen_ref, sems):
    rows, wide = arrived_ref.shape
    width, hid = gate_w.shape
    piece = width // PIECES
    devs = rows // SUB
    extras = devs * EXTRA
    step = pl.program_id(0)
    kc = width // W_CHUNKS
    hc = hid // 2

    def gate_copy(k):
        s = pl.ds(k * kc, kc)
        return pltpu.make_async_copy(gate_hbm.at[s], gate_w.at[s], sems.at[k])

    def up_copy(k):
        s = pl.ds(k * kc, kc)
        return pltpu.make_async_copy(up_hbm.at[s], up_w.at[s], sems.at[W_CHUNKS + k])

    def down_copy(k):
        s = pl.ds(k * hc, hc)
        return pltpu.make_async_copy(down_hbm.at[s], down_w.at[s], sems.at[2 * W_CHUNKS + k])

    @pl.when(step == 0)
    def _():
        for k in range(W_CHUNKS):
            gate_copy(k).start()
            up_copy(k).start()
        for k in range(2):
            down_copy(k).start()
        seen_ref[...] = jnp.zeros_like(seen_ref)

    src = _iota((rows, rows), 0)
    order = (_iota((rows, rows), 1) == (src % extras) * PIECES + src // extras).astype(BF16)
    extra = _dot(order, arrived_ref[:, width:]).astype(BF16)
    x_ref[0:rows, :] = arrived_ref[:, 0:width]
    for c in range(PIECES):
        x_ref[rows : rows + extras, c * piece : (c + 1) * piece] = extra[c * extras : (c + 1) * extras]

    total = rows + extras
    live = (x_ref[:, 0:LANES].astype(F32) < MARK * 0.5).astype(BF16)
    row = _iota((total, total), 0)
    dev = jnp.where(row < rows, row // SUB, (row - rows) // EXTRA)
    col = _iota((total, total), 1)
    col_dev = jnp.where(col < rows, col // SUB, (col - rows) // EXTRA)
    earlier = _dot((col_dev < dev).astype(BF16), live)
    lane_row = _iota((total, LANES), 0)
    slot = jnp.where(lane_row < rows, lane_row % SUB, SUB + (lane_row - rows) % EXTRA)
    position = seen_ref[0:1, :] + earlier + slot.astype(F32)
    kept = (live.astype(F32) > 0) & (position < capacity)
    seen_ref[0:1, :] = seen_ref[0:1, :] + jnp.sum(live.astype(F32), axis=0, keepdims=True)

    @pl.when(step == 0)
    def _():
        for k in range(W_CHUNKS):
            gate_copy(k).wait()
            up_copy(k).wait()
            x = x_ref[:, k * kc : (k + 1) * kc]
            g = _dot(x, gate_w[k * kc : (k + 1) * kc, :])
            u = _dot(x, up_w[k * kc : (k + 1) * kc, :])
            if k == 0:
                g_ref[...] = g
                u_ref[...] = u
            else:
                g_ref[...] += g
                u_ref[...] += u

    @pl.when(step > 0)
    def _():
        g_ref[...] = _dot(x_ref[...], gate_w[...])
        u_ref[...] = _dot(x_ref[...], up_w[...])

    for j in range(hid // LANES):
        s = slice(j * LANES, (j + 1) * LANES)
        g = g_ref[:, s]
        h_ref[:, s] = jnp.where(kept, g / (1.0 + jnp.exp(-g)) * u_ref[:, s], 0.0).astype(BF16)

    @pl.when(step == 0)
    def _():
        for k in range(2):
            down_copy(k).wait()

    out_ref[:, 0:width] = _dot(h_ref[0:rows, :], down_w[...]).astype(BF16)
    extra_out = _dot(h_ref[rows:, :], down_w[...]).astype(BF16)
    stacked = jnp.concatenate([extra_out[:, c * piece : (c + 1) * piece] for c in range(PIECES)], axis=0)
    dst = _iota((rows, rows), 0)
    back = (_iota((rows, rows), 1) == (dst % PIECES) * extras + dst // PIECES).astype(BF16)
    out_ref[:, width:] = _dot(back, stacked).astype(BF16)


def expert(arrived, w_gate, w_up, w_down, capacity):
    total_rows, wide = arrived.shape
    width, hid = w_gate.shape
    rows = 256
    full = rows + rows // SUB * EXTRA
    block = pl.BlockSpec((rows, wide), lambda i: (i, 0))
    anywhere = pl.BlockSpec(memory_space=pl.ANY)

    def body(*refs):
        expert_body(float(capacity), *refs)

    return pl.pallas_call(
        body,
        grid=(total_rows // rows,),
        in_specs=[block, anywhere, anywhere, anywhere],
        out_specs=block,
        out_shape=jax.ShapeDtypeStruct(arrived.shape, BF16),
        scratch_shapes=[
            pltpu.VMEM((width, hid), BF16),
            pltpu.VMEM((width, hid), BF16),
            pltpu.VMEM((hid, width), BF16),
            pltpu.VMEM((full, width), BF16),
            pltpu.VMEM((full, hid), F32),
            pltpu.VMEM((full, hid), F32),
            pltpu.VMEM((full, hid), BF16),
            pltpu.VMEM((8, LANES), F32),
            pltpu.SemaphoreType.DMA((2 * W_CHUNKS + 2,)),
        ],
        compiler_params=pltpu.CompilerParams(vmem_limit_bytes=VMEM_BYTES),
        name="expert",
    )(arrived, w_gate, w_up, w_down)


def combine_body(ids_t_ref, quanta_t_ref, back_ref, out_ref, rank_ref, gate_ref, acc_ref):
    toks, width = out_ref.shape
    rows = back_ref.shape[0]
    experts = rank_ref.shape[1]
    piece = width // PIECES
    step = pl.program_id(0)

    @pl.when(step == 0)
    def _():
        rank_ref[...] = _ranks(_chosen(ids_t_ref, experts)).T.astype(BF16)
        quanta = quanta_t_ref[...].astype(F32)
        scale = ROUTED_SCALE * quanta / jnp.sum(quanta, axis=0, keepdims=True)
        row = _iota((experts, toks), 0)
        gate = jnp.zeros((experts, toks), F32)
        for k in range(ids_t_ref.shape[0]):
            gate = gate + jnp.where(ids_t_ref[k : k + 1, :] == row, scale[k : k + 1, :], 0.0)
        gate = gate.T
        high = gate.astype(BF16)
        gate_ref[0:toks, :] = high
        gate_ref[toks:, :] = (gate - high.astype(F32)).astype(BF16)
        acc_ref[...] = jnp.zeros_like(acc_ref)

    col = _iota((experts, rows), 1) + step * rows
    spread = (col // SUB == _iota((experts, rows), 0)).astype(BF16)
    rank = _dot(rank_ref[...], spread).astype(jnp.int32)
    gate = _dot(gate_ref[...], spread)
    rank = jnp.concatenate([rank, rank], axis=0)
    sub = _iota((2 * toks, rows), 1) % SUB
    acc_ref[...] += _dot(jnp.where(rank == sub, gate, 0.0).astype(BF16), back_ref[:, 0:width])
    extra = jnp.where(rank == SUB + sub // PIECES, gate, 0.0)
    for c in range(PIECES):
        part = jnp.where(sub % PIECES == c, extra, 0.0).astype(BF16)
        acc_ref[:, c * piece : (c + 1) * piece] += _dot(part, back_ref[:, width:])

    @pl.when(step == pl.num_programs(0) - 1)
    def _():
        out_ref[...] = (acc_ref[0:toks, :] + acc_ref[toks:, :]).astype(BF16)


def combine(ids_t, quanta_t, back, experts):
    top, toks = ids_t.shape
    total_rows, wide = back.shape
    width = wide * PIECES // (PIECES + 1)
    rows = 256
    small = pl.BlockSpec((top, toks), lambda i: (0, 0))
    return pl.pallas_call(
        combine_body,
        grid=(total_rows // rows,),
        in_specs=[small, small, pl.BlockSpec((rows, wide), lambda i: (i, 0))],
        out_specs=pl.BlockSpec((toks, width), lambda i: (0, 0)),
        out_shape=jax.ShapeDtypeStruct((toks, width), BF16),
        scratch_shapes=[
            pltpu.VMEM((toks, experts), BF16),
            pltpu.VMEM((2 * toks, experts), BF16),
            pltpu.VMEM((2 * toks, width), F32),
        ],
        compiler_params=pltpu.CompilerParams(vmem_limit_bytes=VMEM_BYTES),
        name="combine",
    )(ids_t, quanta_t, back)


def exchange(rows, experts):
    blocks = rows.reshape(experts, SUB, rows.shape[1])
    blocks = lax.all_to_all(blocks, ("node", "local"), split_axis=0, concat_axis=0, tiled=True)
    return blocks.reshape(rows.shape)


def on_device(tokens, expert_ids, gate_quanta, w_gate, w_up, w_down):
    experts = lax.axis_size("node") * lax.axis_size("local")
    capacity = tokens.shape[0] * expert_ids.shape[1] * 9 // 8
    ids_t = expert_ids.T
    outgoing = dispatch(ids_t, tokens, experts)
    arrived = exchange(outgoing, experts)
    results = expert(arrived, w_gate[0], w_up[0], w_down[0], capacity)
    returned = exchange(results, experts)
    return combine(ids_t, gate_quanta.T, returned, experts)


def solution(mesh):
    rows = P(("node", "local"), None)
    weights = P(("node", "local"), None, None)
    return jax.shard_map(
        on_device,
        mesh=mesh,
        in_specs=(rows, rows, rows, weights, weights, weights),
        out_specs=rows,
        check_vma=False,
    )
```

time: 576 us -> 291 us (0.51)
  the two profiles are of different devices: /device:TPU:84 before, /device:TPU:1 now
where the time goes in v1:
time: 291 us
  blocking collectives  230 us (79%)
  Pallas kernels  60.8 us (21%)
    all_to_all x2, blocking collectives, exchange(): lax.all_to_all(blocks, ('node', 'local'), split_axis=0, concat_axis=0, ti...  230 us
    pallas_call x1, Pallas kernels, expert(): pl.pallas_call(body, grid=(total_rows // rows,), in_specs=[block, anywher...  43.6 us
    pallas_call x1, Pallas kernels, combine(): pl.pallas_call(combine_body, grid=(total_rows // rows,), in_specs=[small,...  9 us
    pallas_call x1, Pallas kernels, dispatch(): pl.pallas_call(dispatch_body, grid=(experts * SUB // rows,), in_specs=[pl...  8.11 us

profile of v1, /device:TPU:1, one launch (start us, length us, event | category | flops | bytes accessed | tf_op | source)
XLA Modules:
  0.0 290.8 jit_solution(10259397514801676598)
XLA Ops:
  0.0 8.1 %dispatch.1 = bf16[1024,4480]{1,0:T(8,128)(2,1)} custom-call(s32[8,128]{1,0:T(8,128)} %bitcast.16, bf16[128,3584]{1,0:T(8,128)(2,1)} %tokens_ref.1), custom_call_target="tpu_custom_call" | custom-call | tf_op jit(solution)/shard_map/dispatch/pallas_call | solution.py:75
  8.1 118.0 %all_to_all.10 = bf16[128,8,4480]{2,1,0:T(8,128)(2,1)} all-to-all(bf16[128,8,4480]{2,1,0:T(8,128)(2,1)} %bitcast.12), channel_id=1, replica_groups=mesh['node'=16,'local'=8] {'node','local'}, dimensions={0} | all-to-all | bytes 18350080 | tf_op jit(solution)/shard_map/all_to_all | solution.py:278
  126.1 43.6 %expert.1 = bf16[1024,4480]{1,0:T(8,128)(2,1)} custom-call(bf16[1024,4480]{1,0:T(8,128)(2,1)} %bitcast.9, bf16[3584,1024]{1,0:T(8,128)(2,1)} %bitcast.13, bf16[3584,1024]{1,0:T(8,128)(2,1)} %bitcast.14, bf16[1024,3584]{1,0:T(8,128)(2,1)} %bitcast.15), custom_call_target="tpu_custom_call" | custom-call | tf_op jit(solution)/shard_map/expert/pallas_call | solution.py:193
  169.8 112.0 %all_to_all.11 = bf16[128,8,4480]{2,1,0:T(8,128)(2,1)} all-to-all(bf16[128,8,4480]{2,1,0:T(8,128)(2,1)} %bitcast.10), channel_id=1, replica_groups=mesh['node'=16,'local'=8] {'node','local'}, dimensions={0} | all-to-all | bytes 18350080 | tf_op jit(solution)/shard_map/all_to_all | solution.py:278
  281.8 9.0 %combine.1 = bf16[128,3584]{1,0:T(8,128)(2,1)} custom-call(s32[8,128]{1,0:T(8,128)} %bitcast.17, s32[8,128]{1,0:T(8,128)} %bitcast.18, bf16[1024,4480]{1,0:T(8,128)(2,1)} %bitcast.11), custom_call_target="tpu_custom_call" | custom-call | tf_op jit(solution)/shard_map/combine/pallas_call | solution.py:260

commit v2 on v0

v2 whole, which is shorter than its diff:
```python
import jax
import jax.numpy as jnp
from jax import lax
from jax.experimental import pallas as pl
from jax.experimental.pallas import tpu as pltpu
from jax.sharding import PartitionSpec as P

AXES = ("node", "local")
ROUTED_SCALE = 2.5
SUB = 8
PARTS_A = ((0, 2), (4, 4))
PARTS_B = ((6, 2),)
LANES = 128
ROWS = 256
VMEM_BYTES = 58 * 1024 * 1024
BF16 = jnp.bfloat16
F32 = jnp.float32


def _iota(shape, dim):
    return lax.broadcasted_iota(jnp.int32, shape, dim)


def _dot(a, b):
    return jnp.dot(a, b, preferred_element_type=F32)


def _params():
    return pltpu.CompilerParams(vmem_limit_bytes=VMEM_BYTES)


def _whole(a):
    return pl.BlockSpec(a.shape, lambda i: (0, 0))


def _columns(parts, width):
    return sum(width // pieces for first, pieces in parts)


def _fill(parts, rank_rep, tokens_ref, out_ref):
    rows, toks = rank_rep.shape
    width = tokens_ref.shape[1]
    sub = _iota((rows, toks), 0) % SUB
    col = 0
    for first, pieces in parts:
        piece = width // pieces
        mine = rank_rep == first + sub // pieces
        acc = None
        for c in range(pieces):
            term = _dot((mine & (sub % pieces == c)).astype(BF16), tokens_ref[:, c * piece : (c + 1) * piece])
            acc = term if acc is None else acc + term
        out_ref[:, col : col + piece] = acc.astype(BF16)
        col += piece


def _spread(rows, experts, step):
    row = _iota((rows, experts), 0) + step * rows
    return (row // SUB == _iota((rows, experts), 1)).astype(BF16)


def dispatch_a_body(ids_t_ref, tokens_ref, out_ref, rank_ref, count_ref):
    experts, toks = rank_ref.shape
    step = pl.program_id(0)

    @pl.when(step == 0)
    def _():
        row = _iota((experts, toks), 0)
        chosen = jnp.zeros((experts, toks), F32)
        for k in range(ids_t_ref.shape[0]):
            chosen = chosen + (ids_t_ref[k : k + 1, :] == row).astype(F32)
        before = (_iota((toks, toks), 0) < _iota((toks, toks), 1)).astype(BF16)
        picked = chosen.astype(BF16)
        rank_ref[...] = jnp.where(chosen > 0, _dot(picked, before), -1.0).astype(BF16)
        count_ref[...] = _dot(picked, jnp.ones((toks, LANES), BF16)).astype(BF16)

    spread = _spread(out_ref.shape[0], experts, step)
    _fill(PARTS_A, _dot(spread, rank_ref[...]).astype(jnp.int32), tokens_ref, out_ref)
    out_ref[:, out_ref.shape[1] - LANES :] = _dot(spread, count_ref[...]).astype(BF16)


def dispatch_a(ids_t, tokens, experts):
    toks, width = tokens.shape
    cols = _columns(PARTS_A, width) + LANES
    return pl.pallas_call(
        dispatch_a_body,
        grid=(experts * SUB // ROWS,),
        in_specs=[_whole(ids_t), _whole(tokens)],
        out_specs=[
            pl.BlockSpec((ROWS, cols), lambda i: (i, 0)),
            pl.BlockSpec((experts, toks), lambda i: (0, 0)),
        ],
        out_shape=[
            jax.ShapeDtypeStruct((experts * SUB, cols), BF16),
            jax.ShapeDtypeStruct((experts, toks), BF16),
        ],
        scratch_shapes=[pltpu.VMEM((experts, LANES), BF16)],
        compiler_params=_params(),
        name="dispatch_a",
    )(ids_t, tokens)


def dispatch_b_body(rank_ref, tokens_ref, out_ref):
    spread = _spread(out_ref.shape[0], rank_ref.shape[0], pl.program_id(0))
    _fill(PARTS_B, _dot(spread, rank_ref[...]).astype(jnp.int32), tokens_ref, out_ref)


def dispatch_b(ranks, tokens):
    experts = ranks.shape[0]
    cols = _columns(PARTS_B, tokens.shape[1])
    return pl.pallas_call(
        dispatch_b_body,
        grid=(experts * SUB // ROWS,),
        in_specs=[_whole(ranks), _whole(tokens)],
        out_specs=pl.BlockSpec((ROWS, cols), lambda i: (i, 0)),
        out_shape=jax.ShapeDtypeStruct((experts * SUB, cols), BF16),
        compiler_params=_params(),
        name="dispatch_b",
    )(ranks, tokens)


def _regroup(pieces, back):
    per = ROWS // pieces
    src, dst = _iota((ROWS, ROWS), 1), _iota((ROWS, ROWS), 0)
    if back:
        src, dst = dst, src
    return (src == (dst % per) * pieces + dst // per).astype(BF16)


def expert_body(parts, capacity, arrived_ref, counts_ref, gate_ref, up_ref, down_ref, out_ref, x_ref, h_ref, y_ref, kept_ref):
    total = counts_ref.shape[0]
    rows, width = x_ref.shape
    cols = gate_ref.shape[1]
    out_cols = down_ref.shape[1]
    steps = h_ref.shape[1] // cols
    i = pl.program_id(0)

    def blocks(pieces, base):
        per = ROWS // pieces
        return [(slice(b * ROWS, (b + 1) * ROWS), base + b * per, per) for b in range(total // ROWS)]

    @pl.when(i == 0)
    def _():
        base, col = 0, 0
        for first, pieces in parts:
            piece, slots = width // pieces, SUB // pieces
            order = _regroup(pieces, False)
            for sub_rows, at, per in blocks(pieces, base):
                sorted_rows = _dot(order, arrived_ref[sub_rows, col : col + piece]).astype(BF16)
                for c in range(pieces):
                    x_ref[at : at + per, c * piece : (c + 1) * piece] = sorted_rows[c * per : (c + 1) * per]
            count = total // pieces
            row, src = _iota((count, total), 0), _iota((count, total), 1)
            earlier = ((src % SUB == 0) & (src // SUB < row // slots)).astype(BF16)
            slot = first + _iota((count, LANES), 0) % slots
            position = _dot(earlier, counts_ref[...]) + slot.astype(F32)
            kept_ref[base : base + count, :] = (position < capacity).astype(F32)
            base, col = base + count, col + piece

    @pl.when(i < steps)
    def _():
        gate = _dot(x_ref[...], gate_ref[...])
        h = 0.5 * gate * (1.0 + jnp.tanh(0.5 * gate)) * _dot(x_ref[...], up_ref[...])
        kept = jnp.concatenate([kept_ref[...]] * (cols // LANES), axis=1)
        h_ref[:, pl.ds(pl.multiple_of(i * cols, LANES), cols)] = jnp.where(kept > 0, h, 0.0).astype(BF16)

    @pl.when(i >= steps)
    def _():
        y = _dot(h_ref[...], down_ref[...]).astype(BF16)
        y_ref[:, pl.ds(pl.multiple_of((i - steps) * out_cols, LANES), out_cols)] = y

    @pl.when(i == pl.num_programs(0) - 1)
    def _():
        base, col = 0, 0
        for first, pieces in parts:
            piece = width // pieces
            order = _regroup(pieces, True)
            for sub_rows, at, per in blocks(pieces, base):
                stacked = [y_ref[at : at + per, c * piece : (c + 1) * piece] for c in range(pieces)]
                out_ref[sub_rows, col : col + piece] = _dot(order, jnp.concatenate(stacked, axis=0)).astype(BF16)
            base, col = base + total // pieces, col + piece


def expert(parts, arrived, counted, w_gate, w_up, w_down, capacity, name):
    total = arrived.shape[0]
    width, hid = w_gate.shape
    rows = sum(total // pieces for first, pieces in parts)
    cols, out_cols = 256, 512
    steps = hid // cols
    out_width = _columns(parts, width)
    counts_at = counted.shape[1] // LANES - 1
    hidden_block = pl.BlockSpec((width, cols), lambda i: (0, jnp.minimum(i, steps - 1)))

    def body(*refs):
        expert_body(parts, float(capacity), *refs)

    return pl.pallas_call(
        body,
        grid=(steps + width // out_cols,),
        in_specs=[
            pl.BlockSpec(arrived.shape, lambda i: (0, 0), pipeline_mode=pl.Buffered(1)),
            pl.BlockSpec((total, LANES), lambda i: (0, counts_at), pipeline_mode=pl.Buffered(1)),
            hidden_block,
            hidden_block,
            pl.BlockSpec((hid, out_cols), lambda i: (0, jnp.maximum(i - steps, 0))),
        ],
        out_specs=pl.BlockSpec((total, out_width), lambda i: (0, 0)),
        out_shape=jax.ShapeDtypeStruct((total, out_width), BF16),
        scratch_shapes=[
            pltpu.VMEM((rows, width), BF16),
            pltpu.VMEM((rows, hid), BF16),
            pltpu.VMEM((rows, width), BF16),
            pltpu.VMEM((rows, LANES), F32),
        ],
        compiler_params=_params(),
        cost_estimate=pl.CostEstimate(
            flops=6 * rows * width * hid, transcendentals=rows * hid, bytes_accessed=6 * width * hid + 4 * rows * width
        ),
        name=name,
    )(arrived, counted, w_gate, w_up, w_down)


def _weights(parts, rank, gate, out_refs):
    toks, experts = rank.shape
    subs = experts * SUB
    spread = (_iota((experts, subs), 1) // SUB == _iota((experts, subs), 0)).astype(BF16)
    rank = _dot(rank, spread).astype(jnp.int32)
    rank = jnp.concatenate([rank, rank], axis=0)
    gate = _dot(gate, spread)
    sub = _iota((2 * toks, subs), 1) % SUB
    for (first, pieces), out_ref in zip(parts, out_refs):
        weight = jnp.where(rank == first + sub // pieces, gate, 0.0)
        for c in range(pieces):
            out_ref[c] = jnp.where(sub % pieces == c, weight, 0.0).astype(BF16)


def _column(i):
    return (i % 2) * 2 + i // 2


def combine_a_body(ids_t_ref, quanta_t_ref, ranks_ref, half_ref, quarter_ref, out_ref, later_ref, half_w, quarter_w):
    toks = out_ref.shape[0]
    experts = ranks_ref.shape[0]
    i = pl.program_id(0)

    @pl.when(i == 0)
    def _():
        rank = ranks_ref[...].astype(F32).T.astype(BF16)
        quanta = quanta_t_ref[...].astype(F32)
        scale = ROUTED_SCALE * quanta / jnp.sum(quanta, axis=0, keepdims=True)
        row = _iota((experts, toks), 0)
        gate = jnp.zeros((experts, toks), F32)
        for k in range(ids_t_ref.shape[0]):
            gate = gate + jnp.where(ids_t_ref[k : k + 1, :] == row, scale[k : k + 1, :], 0.0)
        gate = gate.T
        high = gate.astype(BF16)
        gate = jnp.concatenate([high, (gate - high.astype(F32)).astype(BF16)], axis=0)
        _weights(PARTS_A, rank, gate, (half_w, quarter_w))
        _weights(PARTS_B, rank, gate, (later_ref,))

    total = _dot(half_w[i % 2], half_ref[...]) + _dot(quarter_w[_column(i)], quarter_ref[...])
    out_ref[...] = total[0:toks] + total[toks:]


def combine_a(ids_t, quanta_t, ranks, back, width):
    experts, toks = ranks.shape
    subs = back.shape[0]
    quarter = width // 4
    return pl.pallas_call(
        combine_a_body,
        grid=(4,),
        in_specs=[
            _whole(ids_t),
            _whole(quanta_t),
            _whole(ranks),
            pl.BlockSpec((subs, quarter), lambda i: (0, i // 2)),
            pl.BlockSpec((subs, quarter), lambda i: (0, 2)),
        ],
        out_specs=[
            pl.BlockSpec((toks, quarter), lambda i: (0, _column(i))),
            pl.BlockSpec((2, 2 * toks, subs), lambda i: (0, 0, 0)),
        ],
        out_shape=[
            jax.ShapeDtypeStruct((toks, width), F32),
            jax.ShapeDtypeStruct((2, 2 * toks, subs), BF16),
        ],
        scratch_shapes=[pltpu.VMEM((2, 2 * toks, subs), BF16), pltpu.VMEM((4, 2 * toks, subs), BF16)],
        compiler_params=_params(),
        name="combine_a",
    )(ids_t, quanta_t, ranks, back, back)


def combine_b_body(sum_ref, weight_ref, half_ref, out_ref):
    toks = out_ref.shape[0]
    total = _dot(weight_ref[pl.program_id(0) % 2], half_ref[...])
    out_ref[...] = (sum_ref[...] + total[0:toks] + total[toks:]).astype(BF16)


def combine_b(partial, weight, back):
    toks, width = partial.shape
    quarter = width // 4
    block = pl.BlockSpec((toks, quarter), lambda i: (0, _column(i)))
    return pl.pallas_call(
        combine_b_body,
        grid=(4,),
        in_specs=[
            block,
            pl.BlockSpec(weight.shape, lambda i: (0, 0, 0)),
            pl.BlockSpec((back.shape[0], quarter), lambda i: (0, i // 2)),
        ],
        out_specs=block,
        out_shape=jax.ShapeDtypeStruct((toks, width), BF16),
        compiler_params=_params(),
        name="combine_b",
    )(partial, weight, back)


def exchange(rows):
    blocks = rows.reshape(rows.shape[0] // SUB, SUB, rows.shape[1])
    blocks = lax.all_to_all(blocks, AXES, split_axis=0, concat_axis=0, tiled=True)
    return blocks.reshape(rows.shape)


def on_device(tokens, expert_ids, gate_quanta, w_gate, w_up, w_down):
    experts = lax.axis_size("node") * lax.axis_size("local")
    capacity = tokens.shape[0] * expert_ids.shape[1] * 9 // 8
    ids_t = expert_ids.T
    weights = (w_gate[0], w_up[0], w_down[0])
    out_a, ranks = dispatch_a(ids_t, tokens, experts)
    in_a = exchange(out_a)
    out_b = dispatch_b(ranks, tokens)
    in_a, out_b = lax.optimization_barrier((in_a, out_b))
    in_b = exchange(out_b)
    done_a = expert(PARTS_A, in_a, in_a, *weights, capacity, "expert_a")
    back_a = exchange(done_a)
    done_b = expert(PARTS_B, in_b, in_a, *weights, capacity, "expert_b")
    back_a, done_b = lax.optimization_barrier((back_a, done_b))
    back_b = exchange(done_b)
    partial, weight = combine_a(ids_t, gate_quanta.T, ranks, back_a, tokens.shape[1])
    return combine_b(partial, weight, back_b)


def solution(mesh):
    rows = P(AXES, None)
    weights = P(AXES, None, None)
    return jax.shard_map(
        on_device,
        mesh=mesh,
        in_specs=(rows, rows, rows, weights, weights, weights),
        out_specs=rows,
        check_vma=False,
    )
```

time: 576 us -> 274 us (0.48)
  the two profiles are of different devices: /device:TPU:84 before, /device:TPU:1 now
where the time goes in v2:
time: 274 us; the launch traced here: 273 us
  waiting for transfers between devices  161 us (59%)
  Pallas kernels  84.3 us (31%)
  starting transfers between devices  28.3 us (10%)
    all_to_all x4, waiting for transfers between devices, exchange(): lax.all_to_all(blocks, AXES, split_axis=0, concat_axis=0, tiled=True)  161 us
    pallas_call x2, Pallas kernels, expert(): pl.pallas_call(body, grid=(steps + width // out_cols,), in_specs=[pl.Bloc...  54.8 us
    all_to_all x4, starting transfers between devices, exchange(): lax.all_to_all(blocks, AXES, split_axis=0, concat_axis=0, tiled=True)  28.3 us
    pallas_call x1, Pallas kernels, combine_a(): pl.pallas_call(combine_a_body, grid=(4,), in_specs=[_whole(ids_t), _whole...  9.67 us
    pallas_call x1, Pallas kernels, dispatch_a(): pl.pallas_call(dispatch_a_body, grid=(experts * SUB // ROWS,), in_specs=[...  7.66 us
    pallas_call x1, Pallas kernels, combine_b(): pl.pallas_call(combine_b_body, grid=(4,), in_specs=[block, pl.BlockSpec(w...  6.59 us
    pallas_call x1, Pallas kernels, dispatch_b(): pl.pallas_call(dispatch_b_body, grid=(experts * SUB // ROWS,), in_specs=[...  5.57 us
  transfers between devices with their start and end apart: 4, of which 4 were waited for; matrix products, arithmetic and copies ran while one was open for 0% of the time, Pallas kernels for 26%

profile of v2, /device:TPU:1, one launch (start us, length us, event | category | flops | bytes accessed | tf_op | source)
XLA Modules:
  0.0 273.4 jit_solution(4840354690608466429)
XLA Ops:
  0.0 7.7 %dispatch_a.1 = (bf16[1024,2816]{1,0:T(8,128)(2,1)}, bf16[128,128]{1,0:T(8,128)(2,1)}) custom-call(s32[8,128]{1,0:T(8,128)} %bitcast.17, bf16[128,3584]{1,0:T(8,128)(2,1)} %tokens_ref.3), custom_call_target="tpu_custom_call" | custom-call | tf_op jit(solution)/shard_map/dispatch_a/pallas_call | solution.py:84
  7.7 11.9 %all-to-all-start = ((bf16[128,8,2816]{2,1,0:T(8,128)(2,1)}), bf16[128,8,2816]{2,1,0:T(8,128)(2,1)}, u32[]{:S(2)}, u32[]{:S(2)}) async-start(bf16[128,8,2816]{2,1,0:T(8,128)(2,1)} %bitcast.14), calls=%async_computation | async-start | bytes 11534336 | tf_op jit(solution)/shard_map/all_to_all | solution.py:319
  19.6 5.6 %dispatch_b.1 = bf16[1024,1792]{1,0:T(8,128)(2,1)} custom-call(bf16[128,128]{1,0:T(8,128)(2,1)} %get-tuple-element.13.rank_ref.ranks_ref, bf16[128,3584]{1,0:T(8,128)(2,1)} %tokens_ref.3), custom_call_target="tpu_custom_call" | custom-call | tf_op jit(solution)/shard_map/dispatch_b/pallas_call | solution.py:110
  25.1 64.0 %all-to-all-done = bf16[128,8,2816]{2,1,0:T(8,128)(2,1)} async-done(((bf16[128,8,2816]{2,1,0:T(8,128)(2,1)}), bf16[128,8,2816]{2,1,0:T(8,128)(2,1)}, u32[]{:S(2)}, u32[]{:S(2)}) %all-to-all-start) | async-done | bytes 5767200 | tf_op jit(solution)/shard_map/all_to_all | solution.py:319
  89.2 5.4 %all-to-all-start.2 = ((bf16[128,8,1792]{2,1,0:T(8,128)(2,1)}), bf16[128,8,1792]{2,1,0:T(8,128)(2,1)}, u32[]{:S(2)}, u32[]{:S(2)}) async-start(bf16[128,8,1792]{2,1,0:T(8,128)(2,1)} %bitcast.13), calls=%async_computation.2 | async-start | bytes 7340032 | tf_op jit(solution)/shard_map/all_to_all | solution.py:319
  94.5 31.0 %expert_a.1 = bf16[1024,2688]{1,0:T(8,128)(2,1)} custom-call(bf16[1024,2816]{1,0:T(8,128)(2,1)} %bitcast.3.refs_0_.refs_1_, bf16[1024,2816]{1,0:T(8,128)(2,1)} %bitcast.3.refs_0_.refs_1_, bf16[3584,1024]{1,0:T(8,128)(2,1)} %bitcast.20, bf16[3584,1024]{1,0:T(8,128)(2,1)} %bitcast.22, bf16[1024,3584]{1,0:T(8,128)(2,1)} %bitcast.24), custom_call_target="tpu_custom_call" | custom-call | flops 16911433728 | bytes 33030144 | tf_op jit(solution)/shard_map/expert_a/pallas_call | solution.py:196
  125.5 16.3 %all-to-all-done.2 = bf16[128,8,1792]{2,1,0:T(8,128)(2,1)} async-done(((bf16[128,8,1792]{2,1,0:T(8,128)(2,1)}), bf16[128,8,1792]{2,1,0:T(8,128)(2,1)}, u32[]{:S(2)}, u32[]{:S(2)}) %all-to-all-start.2) | async-done | bytes 3670048 | tf_op jit(solution)/shard_map/all_to_all | solution.py:319
  141.8 5.4 %all-to-all-start.1 = ((bf16[128,8,2688]{2,1,0:T(8,128)(2,1)}), bf16[128,8,2688]{2,1,0:T(8,128)(2,1)}, u32[]{:S(2)}, u32[]{:S(2)}) async-start(bf16[128,8,2688]{2,1,0:T(8,128)(2,1)} %bitcast.15), calls=%async_computation.1 | async-start | bytes 11010048 | tf_op jit(solution)/shard_map/all_to_all | solution.py:319
  147.2 23.8 %expert_b.1 = bf16[1024,1792]{1,0:T(8,128)(2,1)} custom-call(bf16[1024,1792]{1,0:T(8,128)(2,1)} %bitcast.10.refs_0_, bf16[1024,2816]{1,0:T(8,128)(2,1)} %bitcast.3.refs_0_.refs_1_, bf16[3584,1024]{1,0:T(8,128)(2,1)} %bitcast.21, bf16[3584,1024]{1,0:T(8,128)(2,1)} %bitcast.23, bf16[1024,3584]{1,0:T(8,128)(2,1)} %bitcast.25), custom_call_target="tpu_custom_call" | custom-call | flops 11274289152 | bytes 29360128 | tf_op jit(solution)/shard_map/expert_b/pallas_call | solution.py:196
  171.1 42.8 %all-to-all-done.1 = bf16[128,8,2688]{2,1,0:T(8,128)(2,1)} async-done(((bf16[128,8,2688]{2,1,0:T(8,128)(2,1)}), bf16[128,8,2688]{2,1,0:T(8,128)(2,1)}, u32[]{:S(2)}, u32[]{:S(2)}) %all-to-all-start.1) | async-done | bytes 5505056 | tf_op jit(solution)/shard_map/all_to_all | solution.py:319
  213.9 5.6 %all-to-all-start.3 = ((bf16[128,8,1792]{2,1,0:T(8,128)(2,1)}), bf16[128,8,1792]{2,1,0:T(8,128)(2,1)}, u32[]{:S(2)}, u32[]{:S(2)}) async-start(bf16[128,8,1792]{2,1,0:T(8,128)(2,1)} %bitcast.16), calls=%async_computation.3 | async-start | bytes 7340032 | tf_op jit(solution)/shard_map/all_to_all | solution.py:319
  219.5 9.7 %combine_a.1 = (f32[128,3584]{1,0:T(8,128)}, bf16[2,256,1024]{2,1,0:T(8,128)(2,1)}) custom-call(s32[8,128]{1,0:T(8,128)} %bitcast.18, s32[8,128]{1,0:T(8,128)} %bitcast.19, bf16[128,128]{1,0:T(8,128)(2,1)} %get-tuple-element.13.rank_ref.ranks_ref, bf16[1024,2688]{1,0:T(8,128)(2,1)} %bitcast.8.half_ref.quarter_ref, bf16[1024,2688]{1,0:T(8,128)(2,1)} %bitcast.8.half_ref.quarter_ref), custom_call_target="tpu_custom_call" | custom-call | tf_op jit(solution)/shard_map/combine_a/pallas_call | solution.py:268
  229.2 37.6 %all-to-all-done.3 = bf16[128,8,1792]{2,1,0:T(8,128)(2,1)} async-done(((bf16[128,8,1792]{2,1,0:T(8,128)(2,1)}), bf16[128,8,1792]{2,1,0:T(8,128)(2,1)}, u32[]{:S(2)}, u32[]{:S(2)}) %all-to-all-start.3) | async-done | bytes 3670048 | tf_op jit(solution)/shard_map/all_to_all | solution.py:319
  266.8 6.6 %combine_b.1 = bf16[128,3584]{1,0:T(8,128)(2,1)} custom-call(f32[128,3584]{1,0:T(8,128)} %get-tuple-element.18.sum_ref, bf16[2,256,1024]{2,1,0:T(8,128)(2,1)} %get-tuple-element.19.weight_ref, bf16[1024,1792]{1,0:T(8,128)(2,1)} %bitcast.12.half_ref), custom_call_target="tpu_custom_call" | custom-call | tf_op jit(solution)/shard_map/combine_b/pallas_call | solution.py:302
Async XLA Ops:
  7.7 81.5 %all-to-all-start = ((bf16[128,8,2816]{2,1,0:T(8,128)(2,1)}), bf16[128,8,2816]{2,1,0:T(8,128)(2,1)}, u32[]{:S(2)}, u32[]{:S(2)}) async-start(bf16[128,8,2816]{2,1,0:T(8,128)(2,1)} %bitcast.14), calls=%async_computation | async-start | bytes 11534336 | tf_op jit(solution)/shard_map/all_to_all | solution.py:319
  89.2 52.6 %all-to-all-start.2 = ((bf16[128,8,1792]{2,1,0:T(8,128)(2,1)}), bf16[128,8,1792]{2,1,0:T(8,128)(2,1)}, u32[]{:S(2)}, u32[]{:S(2)}) async-start(bf16[128,8,1792]{2,1,0:T(8,128)(2,1)} %bitcast.13), calls=%async_computation.2 | async-start | bytes 7340032 | tf_op jit(solution)/shard_map/all_to_all | solution.py:319
  141.8 72.1 %all-to-all-start.1 = ((bf16[128,8,2688]{2,1,0:T(8,128)(2,1)}), bf16[128,8,2688]{2,1,0:T(8,128)(2,1)}, u32[]{:S(2)}, u32[]{:S(2)}) async-start(bf16[128,8,2688]{2,1,0:T(8,128)(2,1)} %bitcast.15), calls=%async_computation.1 | async-start | bytes 11010048 | tf_op jit(solution)/shard_map/all_to_all | solution.py:319
  213.9 52.9 %all-to-all-start.3 = ((bf16[128,8,1792]{2,1,0:T(8,128)(2,1)}), bf16[128,8,1792]{2,1,0:T(8,128)(2,1)}, u32[]{:S(2)}, u32[]{:S(2)}) async-start(bf16[128,8,1792]{2,1,0:T(8,128)(2,1)} %bitcast.16), calls=%async_computation.3 | async-start | bytes 7340032 | tf_op jit(solution)/shard_map/all_to_all | solution.py:319

commit v3 on v2

--- a/solution.py
+++ b/solution.py
@@ -37,19 +37,26 @@
     return sum(width // pieces for first, pieces in parts)
 
 
-def _fill(parts, rank_rep, tokens_ref, out_ref):
-    rows, toks = rank_rep.shape
-    width = tokens_ref.shape[1]
-    sub = _iota((rows, toks), 0) % SUB
+def _stack(parts, tokens_ref, stack_refs):
+    toks, width = tokens_ref.shape
+    for (first, pieces), stack_ref in zip(parts, stack_refs):
+        piece = width // pieces
+        for c in range(pieces):
+            stack_ref[c * toks : (c + 1) * toks, :] = tokens_ref[:, c * piece : (c + 1) * piece]
+
+
+def _stack_shapes(parts, toks, width):
+    return [pltpu.VMEM((pieces * toks, width // pieces), BF16) for first, pieces in parts]
+
+
+def _fill(parts, rank_rep, stack_refs, out_ref):
+    sub = _iota(rank_rep.shape, 0) % SUB
     col = 0
-    for first, pieces in parts:
-        piece = width // pieces
-        mine = rank_rep == first + sub // pieces
-        acc = None
-        for c in range(pieces):
-            term = _dot((mine & (sub % pieces == c)).astype(BF16), tokens_ref[:, c * piece : (c + 1) * piece])
-            acc = term if acc is None else acc + term
-        out_ref[:, col : col + piece] = acc.astype(BF16)
+    for (first, pieces), stack_ref in zip(parts, stack_refs):
+        mine = jnp.where(rank_rep == first + sub // pieces, sub % pieces, -1)
+        pick = jnp.concatenate([(mine == c).astype(F32) for c in range(pieces)], axis=1).astype(BF16)
+        piece = stack_ref.shape[1]
+        out_ref[:, col : col + piece] = _dot(pick, stack_ref[...]).astype(BF16)
         col += piece
 
 
@@ -58,7 +65,7 @@
     return (row // SUB == _iota((rows, experts), 1)).astype(BF16)
 
 
-def dispatch_a_body(ids_t_ref, tokens_ref, out_ref, rank_ref, count_ref):
+def dispatch_a_body(ids_t_ref, tokens_ref, out_ref, rank_ref, count_ref, *stack_refs):
     experts, toks = rank_ref.shape
     step = pl.program_id(0)
 
@@ -72,9 +79,10 @@
         picked = chosen.astype(BF16)
         rank_ref[...] = jnp.where(chosen > 0, _dot(picked, before), -1.0).astype(BF16)
         count_ref[...] = _dot(picked, jnp.ones((toks, LANES), BF16)).astype(BF16)
+        _stack(PARTS_A, tokens_ref, stack_refs)
 
     spread = _spread(out_ref.shape[0], experts, step)
-    _fill(PARTS_A, _dot(spread, rank_ref[...]).astype(jnp.int32), tokens_ref, out_ref)
+    _fill(PARTS_A, _dot(spread, rank_ref[...]).astype(jnp.int32), stack_refs, out_ref)
     out_ref[:, out_ref.shape[1] - LANES :] = _dot(spread, count_ref[...]).astype(BF16)
 
 
@@ -93,15 +101,19 @@
             jax.ShapeDtypeStruct((experts * SUB, cols), BF16),
             jax.ShapeDtypeStruct((experts, toks), BF16),
         ],
-        scratch_shapes=[pltpu.VMEM((experts, LANES), BF16)],
+        scratch_shapes=[pltpu.VMEM((experts, LANES), BF16), *_stack_shapes(PARTS_A, toks, width)],
         compiler_params=_params(),
         name="dispatch_a",
     )(ids_t, tokens)
 
 
-def dispatch_b_body(rank_ref, tokens_ref, out_ref):
+def dispatch_b_body(rank_ref, tokens_ref, out_ref, *stack_refs):
+    @pl.when(pl.program_id(0) == 0)
+    def _():
+        _stack(PARTS_B, tokens_ref, stack_refs)
+
     spread = _spread(out_ref.shape[0], rank_ref.shape[0], pl.program_id(0))
-    _fill(PARTS_B, _dot(spread, rank_ref[...]).astype(jnp.int32), tokens_ref, out_ref)
+    _fill(PARTS_B, _dot(spread, rank_ref[...]).astype(jnp.int32), stack_refs, out_ref)
 
 
 def dispatch_b(ranks, tokens):
@@ -113,6 +125,7 @@
         in_specs=[_whole(ranks), _whole(tokens)],
         out_specs=pl.BlockSpec((ROWS, cols), lambda i: (i, 0)),
         out_shape=jax.ShapeDtypeStruct((experts * SUB, cols), BF16),
+        scratch_shapes=_stack_shapes(PARTS_B, *tokens.shape),
         compiler_params=_params(),
         name="dispatch_b",
     )(ranks, tokens)
@@ -289,26 +302,49 @@
     )(ids_t, quanta_t, ranks, back, back)
 
 
-def combine_b_body(sum_ref, weight_ref, half_ref, out_ref):
-    toks = out_ref.shape[0]
-    total = _dot(weight_ref[pl.program_id(0) % 2], half_ref[...])
-    out_ref[...] = (sum_ref[...] + total[0:toks] + total[toks:]).astype(BF16)
+def combine_b_body(sum_hbm, weight_hbm, half_hbm, out_hbm, sum_ref, weight_ref, half_ref, out_ref, in_sems, out_sems):
+    toks, quarter = out_ref.shape[1:]
+
+    def columns(q):
+        return pl.ds(q * quarter, quarter)
+
+    weights = [pltpu.make_async_copy(weight_hbm.at[h], weight_ref.at[h], in_sems.at[h]) for h in range(2)]
+    halves = [pltpu.make_async_copy(half_hbm.at[:, columns(h)], half_ref.at[h], in_sems.at[2 + h]) for h in range(2)]
+    sums = [pltpu.make_async_copy(sum_hbm.at[:, columns(q)], sum_ref.at[q], in_sems.at[4 + q]) for q in range(4)]
+    outs = [pltpu.make_async_copy(out_ref.at[q], out_hbm.at[:, columns(q)], out_sems.at[q]) for q in range(4)]
+    for copy in (halves[0], weights[0], sums[0], weights[1], sums[2], halves[1], sums[1], sums[3]):
+        copy.start()
+    for q in (0, 2, 1, 3):
+        h, side = q // 2, q % 2
+        if h == 0:
+            halves[side].wait()
+        if side == 0:
+            weights[h].wait()
+        total = _dot(weight_ref[h], half_ref[side])
+        sums[q].wait()
+        out_ref[q] = (sum_ref[q] + total[0:toks] + total[toks:]).astype(BF16)
+        outs[q].start()
+    for q in range(4):
+        outs[q].wait()
 
 
 def combine_b(partial, weight, back):
     toks, width = partial.shape
     quarter = width // 4
-    block = pl.BlockSpec((toks, quarter), lambda i: (0, _column(i)))
+    anywhere = pl.BlockSpec(memory_space=pl.ANY)
     return pl.pallas_call(
         combine_b_body,
-        grid=(4,),
-        in_specs=[
-            block,
-            pl.BlockSpec(weight.shape, lambda i: (0, 0, 0)),
-            pl.BlockSpec((back.shape[0], quarter), lambda i: (0, i // 2)),
-        ],
-        out_specs=block,
+        in_specs=[anywhere, anywhere, anywhere],
+        out_specs=anywhere,
         out_shape=jax.ShapeDtypeStruct((toks, width), BF16),
+        scratch_shapes=[
+            pltpu.VMEM((4, toks, quarter), F32),
+            pltpu.VMEM(weight.shape, BF16),
+            pltpu.VMEM((2, back.shape[0], quarter), BF16),
+            pltpu.VMEM((4, toks, quarter), BF16),
+            pltpu.SemaphoreType.DMA((8,)),
+            pltpu.SemaphoreType.DMA((4,)),
+        ],
         compiler_params=_params(),
         name="combine_b",
     )(partial, weight, back)

time: 274 us -> 272 us (level)
  Pallas kernels: 84.3 us -> 80.9 us
where the time goes in v3:
time: 272 us; the launch traced here: 271 us
  waiting for transfers between devices  162 us (60%)
  Pallas kernels  80.9 us (30%)
  starting transfers between devices  28.3 us (10%)
    all_to_all x4, waiting for transfers between devices, exchange(): lax.all_to_all(blocks, AXES, split_axis=0, concat_axis=0, tiled=True)  162 us
    pallas_call x2, Pallas kernels, expert(): pl.pallas_call(body, grid=(steps + width // out_cols,), in_specs=[pl.Bloc...  54.8 us
    all_to_all x4, starting transfers between devices, exchange(): lax.all_to_all(blocks, AXES, split_axis=0, concat_axis=0, tiled=True)  28.3 us
    pallas_call x1, Pallas kernels, combine_a(): pl.pallas_call(combine_a_body, grid=(4,), in_specs=[_whole(ids_t), _whole...  9.66 us
    pallas_call x1, Pallas kernels, dispatch_a(): pl.pallas_call(dispatch_a_body, grid=(experts * SUB // ROWS,), in_specs=[...  6.32 us
  transfers between devices with their start and end apart: 4, of which 4 were waited for; matrix products, arithmetic and copies ran while one was open for 0% of the time, Pallas kernels for 26%

profile of v3, /device:TPU:1, one launch (start us, length us, event | category | flops | bytes accessed | tf_op | source)
XLA Modules:
  0.0 271.0 jit_solution(4659980347875361319)
XLA Ops:
  0.0 6.3 %dispatch_a.1 = (bf16[1024,2816]{1,0:T(8,128)(2,1)}, bf16[128,128]{1,0:T(8,128)(2,1)}) custom-call(s32[8,128]{1,0:T(8,128)} %bitcast.17, bf16[128,3584]{1,0:T(8,128)(2,1)} %tokens_ref.3), custom_call_target="tpu_custom_call" | custom-call | tf_op jit(solution)/shard_map/dispatch_a/pallas_call | solution.py:92
  6.3 11.9 %all-to-all-start = ((bf16[128,8,2816]{2,1,0:T(8,128)(2,1)}), bf16[128,8,2816]{2,1,0:T(8,128)(2,1)}, u32[]{:S(2)}, u32[]{:S(2)}) async-start(bf16[128,8,2816]{2,1,0:T(8,128)(2,1)} %bitcast.14), calls=%async_computation | async-start | bytes 11534336 | tf_op jit(solution)/shard_map/all_to_all | solution.py:355
  18.2 4.8 %dispatch_b.1 = bf16[1024,1792]{1,0:T(8,128)(2,1)} custom-call(bf16[128,128]{1,0:T(8,128)(2,1)} %get-tuple-element.13.rank_ref.ranks_ref, bf16[128,3584]{1,0:T(8,128)(2,1)} %tokens_ref.3), custom_call_target="tpu_custom_call" | custom-call | tf_op jit(solution)/shard_map/dispatch_b/pallas_call | solution.py:122
  23.0 64.8 %all-to-all-done = bf16[128,8,2816]{2,1,0:T(8,128)(2,1)} async-done(((bf16[128,8,2816]{2,1,0:T(8,128)(2,1)}), bf16[128,8,2816]{2,1,0:T(8,128)(2,1)}, u32[]{:S(2)}, u32[]{:S(2)}) %all-to-all-start) | async-done | bytes 5767200 | tf_op jit(solution)/shard_map/all_to_all | solution.py:355
  87.8 5.4 %all-to-all-start.2 = ((bf16[128,8,1792]{2,1,0:T(8,128)(2,1)}), bf16[128,8,1792]{2,1,0:T(8,128)(2,1)}, u32[]{:S(2)}, u32[]{:S(2)}) async-start(bf16[128,8,1792]{2,1,0:T(8,128)(2,1)} %bitcast.13), calls=%async_computation.2 | async-start | bytes 7340032 | tf_op jit(solution)/shard_map/all_to_all | solution.py:355
  93.2 31.0 %expert_a.1 = bf16[1024,2688]{1,0:T(8,128)(2,1)} custom-call(bf16[1024,2816]{1,0:T(8,128)(2,1)} %bitcast.3.refs_0_.refs_1_, bf16[1024,2816]{1,0:T(8,128)(2,1)} %bitcast.3.refs_0_.refs_1_, bf16[3584,1024]{1,0:T(8,128)(2,1)} %bitcast.20, bf16[3584,1024]{1,0:T(8,128)(2,1)} %bitcast.22, bf16[1024,3584]{1,0:T(8,128)(2,1)} %bitcast.24), custom_call_target="tpu_custom_call" | custom-call | flops 16911433728 | bytes 33030144 | tf_op jit(solution)/shard_map/expert_a/pallas_call | solution.py:209
  124.2 16.3 %all-to-all-done.2 = bf16[128,8,1792]{2,1,0:T(8,128)(2,1)} async-done(((bf16[128,8,1792]{2,1,0:T(8,128)(2,1)}), bf16[128,8,1792]{2,1,0:T(8,128)(2,1)}, u32[]{:S(2)}, u32[]{:S(2)}) %all-to-all-start.2) | async-done | bytes 3670048 | tf_op jit(solution)/shard_map/all_to_all | solution.py:355
  140.5 5.4 %all-to-all-start.1 = ((bf16[128,8,2688]{2,1,0:T(8,128)(2,1)}), bf16[128,8,2688]{2,1,0:T(8,128)(2,1)}, u32[]{:S(2)}, u32[]{:S(2)}) async-start(bf16[128,8,2688]{2,1,0:T(8,128)(2,1)} %bitcast.15), calls=%async_computation.1 | async-start | bytes 11010048 | tf_op jit(solution)/shard_map/all_to_all | solution.py:355
  145.9 23.8 %expert_b.1 = bf16[1024,1792]{1,0:T(8,128)(2,1)} custom-call(bf16[1024,1792]{1,0:T(8,128)(2,1)} %bitcast.10.refs_0_, bf16[1024,2816]{1,0:T(8,128)(2,1)} %bitcast.3.refs_0_.refs_1_, bf16[3584,1024]{1,0:T(8,128)(2,1)} %bitcast.21, bf16[3584,1024]{1,0:T(8,128)(2,1)} %bitcast.23, bf16[1024,3584]{1,0:T(8,128)(2,1)} %bitcast.25), custom_call_target="tpu_custom_call" | custom-call | flops 11274289152 | bytes 29360128 | tf_op jit(solution)/shard_map/expert_b/pallas_call | solution.py:209
  169.7 42.8 %all-to-all-done.1 = bf16[128,8,2688]{2,1,0:T(8,128)(2,1)} async-done(((bf16[128,8,2688]{2,1,0:T(8,128)(2,1)}), bf16[128,8,2688]{2,1,0:T(8,128)(2,1)}, u32[]{:S(2)}, u32[]{:S(2)}) %all-to-all-start.1) | async-done | bytes 5505056 | tf_op jit(solution)/shard_map/all_to_all | solution.py:355
  212.6 5.6 %all-to-all-start.3 = ((bf16[128,8,1792]{2,1,0:T(8,128)(2,1)}), bf16[128,8,1792]{2,1,0:T(8,128)(2,1)}, u32[]{:S(2)}, u32[]{:S(2)}) async-start(bf16[128,8,1792]{2,1,0:T(8,128)(2,1)} %bitcast.16), calls=%async_computation.3 | async-start | bytes 7340032 | tf_op jit(solution)/shard_map/all_to_all | solution.py:355
  218.2 9.7 %combine_a.1 = (f32[128,3584]{1,0:T(8,128)}, bf16[2,256,1024]{2,1,0:T(8,128)(2,1)}) custom-call(s32[8,128]{1,0:T(8,128)} %bitcast.18, s32[8,128]{1,0:T(8,128)} %bitcast.19, bf16[128,128]{1,0:T(8,128)(2,1)} %get-tuple-element.13.rank_ref.ranks_ref, bf16[1024,2688]{1,0:T(8,128)(2,1)} %bitcast.8.half_ref.quarter_ref, bf16[1024,2688]{1,0:T(8,128)(2,1)} %bitcast.8.half_ref.quarter_ref), custom_call_target="tpu_custom_call" | custom-call | tf_op jit(solution)/shard_map/combine_a/pallas_call | solution.py:281
  227.9 37.6 %all-to-all-done.3 = bf16[128,8,1792]{2,1,0:T(8,128)(2,1)} async-done(((bf16[128,8,1792]{2,1,0:T(8,128)(2,1)}), bf16[128,8,1792]{2,1,0:T(8,128)(2,1)}, u32[]{:S(2)}, u32[]{:S(2)}) %all-to-all-start.3) | async-done | bytes 3670048 | tf_op jit(solution)/shard_map/all_to_all | solution.py:355
  265.5 5.4 %combine_b.1 = bf16[128,3584]{1,0:T(8,128)(2,1)} custom-call(f32[128,3584]{1,0:T(8,128)} %get-tuple-element.18.sum_hbm, bf16[2,256,1024]{2,1,0:T(8,128)(2,1)} %get-tuple-element.19.weight_hbm, bf16[1024,1792]{1,0:T(8,128)(2,1)} %bitcast.12.half_hbm), custom_call_target="tpu_custom_call" | custom-call | tf_op jit(solution)/shard_map/combine_b/pallas_call | solution.py:335
Async XLA Ops:
  6.3 81.5 %all-to-all-start = ((bf16[128,8,2816]{2,1,0:T(8,128)(2,1)}), bf16[128,8,2816]{2,1,0:T(8,128)(2,1)}, u32[]{:S(2)}, u32[]{:S(2)}) async-start(bf16[128,8,2816]{2,1,0:T(8,128)(2,1)} %bitcast.14), calls=%async_computation | async-start | bytes 11534336 | tf_op jit(solution)/shard_map/all_to_all | solution.py:355
  87.8 52.6 %all-to-all-start.2 = ((bf16[128,8,1792]{2,1,0:T(8,128)(2,1)}), bf16[128,8,1792]{2,1,0:T(8,128)(2,1)}, u32[]{:S(2)}, u32[]{:S(2)}) async-start(bf16[128,8,1792]{2,1,0:T(8,128)(2,1)} %bitcast.13), calls=%async_computation.2 | async-start | bytes 7340032 | tf_op jit(solution)/shard_map/all_to_all | solution.py:355
  140.5 72.1 %all-to-all-start.1 = ((bf16[128,8,2688]{2,1,0:T(8,128)(2,1)}), bf16[128,8,2688]{2,1,0:T(8,128)(2,1)}, u32[]{:S(2)}, u32[]{:S(2)}) async-start(bf16[128,8,2688]{2,1,0:T(8,128)(2,1)} %bitcast.15), calls=%async_computation.1 | async-start | bytes 11010048 | tf_op jit(solution)/shard_map/all_to_all | solution.py:355
  212.6 52.9 %all-to-all-start.3 = ((bf16[128,8,1792]{2,1,0:T(8,128)(2,1)}), bf16[128,8,1792]{2,1,0:T(8,128)(2,1)}, u32[]{:S(2)}, u32[]{:S(2)}) async-start(bf16[128,8,1792]{2,1,0:T(8,128)(2,1)} %bitcast.16), calls=%async_computation.3 | async-start | bytes 7340032 | tf_op jit(solution)/shard_map/all_to_all | solution.py:355

commit v4 on v3

--- a/solution.py
+++ b/solution.py
@@ -12,6 +12,7 @@
 PARTS_B = ((6, 2),)
 LANES = 128
 ROWS = 256
+DISPATCH_ROWS = 512
 VMEM_BYTES = 58 * 1024 * 1024
 BF16 = jnp.bfloat16
 F32 = jnp.float32
@@ -91,10 +92,10 @@
     cols = _columns(PARTS_A, width) + LANES
     return pl.pallas_call(
         dispatch_a_body,
-        grid=(experts * SUB // ROWS,),
+        grid=(experts * SUB // DISPATCH_ROWS,),
         in_specs=[_whole(ids_t), _whole(tokens)],
         out_specs=[
-            pl.BlockSpec((ROWS, cols), lambda i: (i, 0)),
+            pl.BlockSpec((DISPATCH_ROWS, cols), lambda i: (i, 0)),
             pl.BlockSpec((experts, toks), lambda i: (0, 0)),
         ],
         out_shape=[
@@ -121,9 +122,9 @@
     cols = _columns(PARTS_B, tokens.shape[1])
     return pl.pallas_call(
         dispatch_b_body,
-        grid=(experts * SUB // ROWS,),
+        grid=(experts * SUB // DISPATCH_ROWS,),
         in_specs=[_whole(ranks), _whole(tokens)],
-        out_specs=pl.BlockSpec((ROWS, cols), lambda i: (i, 0)),
+        out_specs=pl.BlockSpec((DISPATCH_ROWS, cols), lambda i: (i, 0)),
         out_shape=jax.ShapeDtypeStruct((experts * SUB, cols), BF16),
         scratch_shapes=_stack_shapes(PARTS_B, *tokens.shape),
         compiler_params=_params(),
@@ -308,22 +309,21 @@
     def columns(q):
         return pl.ds(q * quarter, quarter)
 
-    weights = [pltpu.make_async_copy(weight_hbm.at[h], weight_ref.at[h], in_sems.at[h]) for h in range(2)]
+    weights = pltpu.make_async_copy(weight_hbm, weight_ref, in_sems.at[0])
     halves = [pltpu.make_async_copy(half_hbm.at[:, columns(h)], half_ref.at[h], in_sems.at[2 + h]) for h in range(2)]
     sums = [pltpu.make_async_copy(sum_hbm.at[:, columns(q)], sum_ref.at[q], in_sems.at[4 + q]) for q in range(4)]
     outs = [pltpu.make_async_copy(out_ref.at[q], out_hbm.at[:, columns(q)], out_sems.at[q]) for q in range(4)]
-    for copy in (halves[0], weights[0], sums[0], weights[1], sums[2], halves[1], sums[1], sums[3]):
+    for copy in (weights, halves[0], sums[0], sums[2], halves[1], sums[1], sums[3]):
         copy.start()
-    for q in (0, 2, 1, 3):
-        h, side = q // 2, q % 2
-        if h == 0:
-            halves[side].wait()
-        if side == 0:
-            weights[h].wait()
-        total = _dot(weight_ref[h], half_ref[side])
-        sums[q].wait()
-        out_ref[q] = (sum_ref[q] + total[0:toks] + total[toks:]).astype(BF16)
-        outs[q].start()
+    weights.wait()
+    for side in range(2):
+        halves[side].wait()
+        total = _dot(weight_ref[...], half_ref[side])
+        for h in range(2):
+            q, at = 2 * h + side, 2 * h * toks
+            sums[q].wait()
+            out_ref[q] = (sum_ref[q] + total[at : at + toks] + total[at + toks : at + 2 * toks]).astype(BF16)
+            outs[q].start()
     for q in range(4):
         outs[q].wait()
 
@@ -331,6 +331,7 @@
 def combine_b(partial, weight, back):
     toks, width = partial.shape
     quarter = width // 4
+    weight = weight.reshape(4 * toks, back.shape[0])
     anywhere = pl.BlockSpec(memory_space=pl.ANY)
     return pl.pallas_call(
         combine_b_body,

time: 272 us -> 271 us (level)
  transfers between devices with their start and end apart: 4 -> 4, of which waited for: 4 -> 4; matrix products, arithmetic and copies ran while one was open for 0% -> 0% of each run, Pallas kernels for 26% -> 25%
where the time goes in v4:
time: 271 us
  waiting for transfers between devices  162 us (60%)
  Pallas kernels  80.1 us (30%)
  starting transfers between devices  28.3 us (10%)
    all_to_all x4, waiting for transfers between devices, exchange(): lax.all_to_all(blocks, AXES, split_axis=0, concat_axis=0, tiled=True)  162 us
    pallas_call x2, Pallas kernels, expert(): pl.pallas_call(body, grid=(steps + width // out_cols,), in_specs=[pl.Bloc...  54.8 us
    all_to_all x4, starting transfers between devices, exchange(): lax.all_to_all(blocks, AXES, split_axis=0, concat_axis=0, tiled=True)  28.3 us
    pallas_call x1, Pallas kernels, combine_a(): pl.pallas_call(combine_a_body, grid=(4,), in_specs=[_whole(ids_t), _whole...  9.66 us
    pallas_call x1, Pallas kernels, dispatch_a(): pl.pallas_call(dispatch_a_body, grid=(experts * SUB // DISPATCH_ROWS,), i...  6.04 us
  transfers between devices with their start and end apart: 4, of which 4 were waited for; matrix products, arithmetic and copies ran while one was open for 0% of the time, Pallas kernels for 25%

profile of v4, /device:TPU:1, one launch (start us, length us, event | category | flops | bytes accessed | tf_op | source)
XLA Modules:
  0.0 270.6 jit_solution(16483300640368199351)
XLA Ops:
  0.0 6.0 %dispatch_a.1 = (bf16[1024,2816]{1,0:T(8,128)(2,1)}, bf16[128,128]{1,0:T(8,128)(2,1)}) custom-call(s32[8,128]{1,0:T(8,128)} %bitcast.19, bf16[128,3584]{1,0:T(8,128)(2,1)} %tokens_ref.3), custom_call_target="tpu_custom_call" | custom-call | tf_op jit(solution)/shard_map/dispatch_a/pallas_call | solution.py:93
  6.0 11.9 %all-to-all-start = ((bf16[128,8,2816]{2,1,0:T(8,128)(2,1)}), bf16[128,8,2816]{2,1,0:T(8,128)(2,1)}, u32[]{:S(2)}, u32[]{:S(2)}) async-start(bf16[128,8,2816]{2,1,0:T(8,128)(2,1)} %bitcast.15), calls=%async_computation | async-start | bytes 11534336 | tf_op jit(solution)/shard_map/all_to_all | solution.py:356
  17.9 4.3 %dispatch_b.1 = bf16[1024,1792]{1,0:T(8,128)(2,1)} custom-call(bf16[128,128]{1,0:T(8,128)(2,1)} %get-tuple-element.13.rank_ref.ranks_ref, bf16[128,3584]{1,0:T(8,128)(2,1)} %tokens_ref.3), custom_call_target="tpu_custom_call" | custom-call | tf_op jit(solution)/shard_map/dispatch_b/pallas_call | solution.py:123
  22.2 65.3 %all-to-all-done = bf16[128,8,2816]{2,1,0:T(8,128)(2,1)} async-done(((bf16[128,8,2816]{2,1,0:T(8,128)(2,1)}), bf16[128,8,2816]{2,1,0:T(8,128)(2,1)}, u32[]{:S(2)}, u32[]{:S(2)}) %all-to-all-start) | async-done | bytes 5767200 | tf_op jit(solution)/shard_map/all_to_all | solution.py:356
  87.6 5.4 %all-to-all-start.2 = ((bf16[128,8,1792]{2,1,0:T(8,128)(2,1)}), bf16[128,8,1792]{2,1,0:T(8,128)(2,1)}, u32[]{:S(2)}, u32[]{:S(2)}) async-start(bf16[128,8,1792]{2,1,0:T(8,128)(2,1)} %bitcast.14), calls=%async_computation.2 | async-start | bytes 7340032 | tf_op jit(solution)/shard_map/all_to_all | solution.py:356
  92.9 31.0 %expert_a.1 = bf16[1024,2688]{1,0:T(8,128)(2,1)} custom-call(bf16[1024,2816]{1,0:T(8,128)(2,1)} %bitcast.3.refs_0_.refs_1_, bf16[1024,2816]{1,0:T(8,128)(2,1)} %bitcast.3.refs_0_.refs_1_, bf16[3584,1024]{1,0:T(8,128)(2,1)} %bitcast.22, bf16[3584,1024]{1,0:T(8,128)(2,1)} %bitcast.24, bf16[1024,3584]{1,0:T(8,128)(2,1)} %bitcast.26), custom_call_target="tpu_custom_call" | custom-call | flops 16911433728 | bytes 33030144 | tf_op jit(solution)/shard_map/expert_a/pallas_call | solution.py:210
  123.9 16.3 %all-to-all-done.2 = bf16[128,8,1792]{2,1,0:T(8,128)(2,1)} async-done(((bf16[128,8,1792]{2,1,0:T(8,128)(2,1)}), bf16[128,8,1792]{2,1,0:T(8,128)(2,1)}, u32[]{:S(2)}, u32[]{:S(2)}) %all-to-all-start.2) | async-done | bytes 3670048 | tf_op jit(solution)/shard_map/all_to_all | solution.py:356
  140.2 5.4 %all-to-all-start.1 = ((bf16[128,8,2688]{2,1,0:T(8,128)(2,1)}), bf16[128,8,2688]{2,1,0:T(8,128)(2,1)}, u32[]{:S(2)}, u32[]{:S(2)}) async-start(bf16[128,8,2688]{2,1,0:T(8,128)(2,1)} %bitcast.16), calls=%async_computation.1 | async-start | bytes 11010048 | tf_op jit(solution)/shard_map/all_to_all | solution.py:356
  145.6 23.8 %expert_b.1 = bf16[1024,1792]{1,0:T(8,128)(2,1)} custom-call(bf16[1024,1792]{1,0:T(8,128)(2,1)} %bitcast.10.refs_0_, bf16[1024,2816]{1,0:T(8,128)(2,1)} %bitcast.3.refs_0_.refs_1_, bf16[3584,1024]{1,0:T(8,128)(2,1)} %bitcast.23, bf16[3584,1024]{1,0:T(8,128)(2,1)} %bitcast.25, bf16[1024,3584]{1,0:T(8,128)(2,1)} %bitcast.27), custom_call_target="tpu_custom_call" | custom-call | flops 11274289152 | bytes 29360128 | tf_op jit(solution)/shard_map/expert_b/pallas_call | solution.py:210
  169.4 42.8 %all-to-all-done.1 = bf16[128,8,2688]{2,1,0:T(8,128)(2,1)} async-done(((bf16[128,8,2688]{2,1,0:T(8,128)(2,1)}), bf16[128,8,2688]{2,1,0:T(8,128)(2,1)}, u32[]{:S(2)}, u32[]{:S(2)}) %all-to-all-start.1) | async-done | bytes 5505056 | tf_op jit(solution)/shard_map/all_to_all | solution.py:356
  212.3 5.6 %all-to-all-start.3 = ((bf16[128,8,1792]{2,1,0:T(8,128)(2,1)}), bf16[128,8,1792]{2,1,0:T(8,128)(2,1)}, u32[]{:S(2)}, u32[]{:S(2)}) async-start(bf16[128,8,1792]{2,1,0:T(8,128)(2,1)} %bitcast.17), calls=%async_computation.3 | async-start | bytes 7340032 | tf_op jit(solution)/shard_map/all_to_all | solution.py:356
  217.9 9.7 %combine_a.1 = (f32[128,3584]{1,0:T(8,128)}, bf16[2,256,1024]{2,1,0:T(8,128)(2,1)}) custom-call(s32[8,128]{1,0:T(8,128)} %bitcast.20, s32[8,128]{1,0:T(8,128)} %bitcast.21, bf16[128,128]{1,0:T(8,128)(2,1)} %get-tuple-element.13.rank_ref.ranks_ref, bf16[1024,2688]{1,0:T(8,128)(2,1)} %bitcast.8.half_ref.quarter_ref, bf16[1024,2688]{1,0:T(8,128)(2,1)} %bitcast.8.half_ref.quarter_ref), custom_call_target="tpu_custom_call" | custom-call | tf_op jit(solution)/shard_map/combine_a/pallas_call | solution.py:282
  227.6 37.6 %all-to-all-done.3 = bf16[128,8,1792]{2,1,0:T(8,128)(2,1)} async-done(((bf16[128,8,1792]{2,1,0:T(8,128)(2,1)}), bf16[128,8,1792]{2,1,0:T(8,128)(2,1)}, u32[]{:S(2)}, u32[]{:S(2)}) %all-to-all-start.3) | async-done | bytes 3670048 | tf_op jit(solution)/shard_map/all_to_all | solution.py:356
  265.2 5.3 %combine_b.1 = bf16[128,3584]{1,0:T(8,128)(2,1)} custom-call(f32[128,3584]{1,0:T(8,128)} %get-tuple-element.18.sum_hbm, bf16[512,1024]{1,0:T(8,128)(2,1)} %bitcast.18, bf16[1024,1792]{1,0:T(8,128)(2,1)} %bitcast.13.half_hbm), custom_call_target="tpu_custom_call" | custom-call | tf_op jit(solution)/shard_map/combine_b/pallas_call | solution.py:336
Async XLA Ops:
  6.0 81.5 %all-to-all-start = ((bf16[128,8,2816]{2,1,0:T(8,128)(2,1)}), bf16[128,8,2816]{2,1,0:T(8,128)(2,1)}, u32[]{:S(2)}, u32[]{:S(2)}) async-start(bf16[128,8,2816]{2,1,0:T(8,128)(2,1)} %bitcast.15), calls=%async_computation | async-start | bytes 11534336 | tf_op jit(solution)/shard_map/all_to_all | solution.py:356
  87.6 52.6 %all-to-all-start.2 = ((bf16[128,8,1792]{2,1,0:T(8,128)(2,1)}), bf16[128,8,1792]{2,1,0:T(8,128)(2,1)}, u32[]{:S(2)}, u32[]{:S(2)}) async-start(bf16[128,8,1792]{2,1,0:T(8,128)(2,1)} %bitcast.14), calls=%async_computation.2 | async-start | bytes 7340032 | tf_op jit(solution)/shard_map/all_to_all | solution.py:356
  140.2 72.1 %all-to-all-start.1 = ((bf16[128,8,2688]{2,1,0:T(8,128)(2,1)}), bf16[128,8,2688]{2,1,0:T(8,128)(2,1)}, u32[]{:S(2)}, u32[]{:S(2)}) async-start(bf16[128,8,2688]{2,1,0:T(8,128)(2,1)} %bitcast.16), calls=%async_computation.1 | async-start | bytes 11010048 | tf_op jit(solution)/shard_map/all_to_all | solution.py:356
  212.3 52.9 %all-to-all-start.3 = ((bf16[128,8,1792]{2,1,0:T(8,128)(2,1)}), bf16[128,8,1792]{2,1,0:T(8,128)(2,1)}, u32[]{:S(2)}, u32[]{:S(2)}) async-start(bf16[128,8,1792]{2,1,0:T(8,128)(2,1)} %bitcast.17), calls=%async_computation.3 | async-start | bytes 7340032 | tf_op jit(solution)/shard_map/all_to_all | solution.py:356
